TPU v7x, 32 devices: a whole 2x2x4 slice. The times are simulated.
32 devices in a mesh: band: 4 (over x, core), grid: 8 (over z, y).
Axes of the slice: x: 2, y: 2, z: 4, core: 2. Of those that a mesh axis runs over, the one named last changes fastest.
Arguments:
- states: float32 [64, 64, 8, 128], P('band', 'grid'), may hold values from -6 to 6
- potential: float32 [64, 8, 128], P('grid'), may hold values from -1 to 1
- proj_index: int32 [16, 128], replicated, may hold values from 0 to 65535, as said below
- proj_value: float32 [16, 128], replicated, may hold values from 0 to 1
- proj_strength: float32 [16], replicated, may hold values from 0.5 to 4
Outputs:
- filtered: float32 [64, 64, 8, 128], P('band', 'grid')
- gram: float32 [64, 64], P('band')
- hamiltonian: float32 [64, 64], P('band')
Inputs may be any that keep to these rules, and one draw needn't show every extreme that they name: `proj_index`: along the first grid dimension every support point lies within 8 planes of its atom's centre plane.
All inputs are finite; a program needn't handle non-finite values.
Results may differ from a plain program's by a relative error of at most 0.0001.
Values sent between devices are 32-bit elements; how exact they have to be, the bound alone decides.
A program may use at most 64 MiB of HBM per device.

v0:
```python
import jax
import jax.numpy as jnp
from jax import lax
from jax.sharding import PartitionSpec as P

RADIUS = 4
DEGREE = 4
stencil_weights = (-205.0 / 72.0, 1.6, -0.2, 8.0 / 315.0, -1.0 / 560.0)
filter_centre = 10.0
filter_half = 6.0


def padded_2(block, sides, width):
    for axis, dim in sides:
        count = lax.axis_size(axis)
        forward = [(i, i + 1) for i in range(count - 1)]
        backward = [(target, source) for source, target in forward]
        low = lax.ppermute(
            lax.slice_in_dim(block, block.shape[dim] - width, None, axis=dim), axis, forward
        )
        high = lax.ppermute(lax.slice_in_dim(block, 0, width, axis=dim), axis, backward)
        block = jnp.concatenate([low, block, high], axis=dim)
    return block


def kinetic(padded):
    extent = padded.shape[-3] - 2 * RADIUS
    middle = padded[..., RADIUS : RADIUS + extent, :, :]
    grid_rows = middle.shape[-2]
    grid_cols = middle.shape[-1]
    pad_widths = [(0, 0)] * (middle.ndim - 2) + [(RADIUS, RADIUS), (RADIUS, RADIUS)]
    padded_yz = jnp.pad(middle, pad_widths)
    summed = 3.0 * stencil_weights[0] * middle
    for shift_by in range(1, RADIUS + 1):
        neighbours = (
            padded[..., RADIUS + shift_by : RADIUS + shift_by + extent, :, :]
            + padded[..., RADIUS - shift_by : RADIUS - shift_by + extent, :, :]
        )
        neighbours = (
            neighbours
            + padded_yz[
                ..., RADIUS + shift_by : RADIUS + shift_by + grid_rows, RADIUS : RADIUS + grid_cols
            ]
            + padded_yz[
                ..., RADIUS - shift_by : RADIUS - shift_by + grid_rows, RADIUS : RADIUS + grid_cols
            ]
        )
        neighbours = (
            neighbours
            + padded_yz[
                ..., RADIUS : RADIUS + grid_rows, RADIUS + shift_by : RADIUS + shift_by + grid_cols
            ]
            + padded_yz[
                ..., RADIUS : RADIUS + grid_rows, RADIUS - shift_by : RADIUS - shift_by + grid_cols
            ]
        )
        summed = summed + stencil_weights[shift_by] * neighbours
    return -0.5 * summed


def inner_rows(left, right):
    return lax.dot_general(
        left,
        right,
        (((1,), (1,)), ((), ())),
        precision=lax.Precision.HIGHEST,
        preferred_element_type=jnp.float32,
    )


def per_device(states, potential, proj_index, proj_value, proj_strength):
    state_count, planes, grid_rows, grid_cols = states.shape
    points = planes * grid_rows * grid_cols
    atom_count = proj_index.shape[0]
    offset = lax.axis_index("grid") * points
    local_idx = proj_index - offset
    inside = (local_idx >= 0) & (local_idx < points)
    safe_idx = jnp.where(inside, local_idx, 0)
    weights = jnp.where(inside, proj_value, 0.0)
    atom_rows = jnp.broadcast_to(jnp.arange(atom_count, dtype=jnp.int32)[:, None], safe_idx.shape)
    projector = jnp.zeros((atom_count, points), jnp.float32).at[atom_rows, safe_idx].add(weights)

    def apply_h(field):
        padded = padded_2(field, (("grid", 1),), RADIUS)
        kinetic_v = kinetic(padded)
        flat_v = field.reshape(state_count, points)
        partial_value = inner_rows(flat_v, projector)
        coeffs = lax.psum(partial_value, "grid")
        scaled = coeffs * proj_strength[None, :]
        nonlocal_v = jnp.dot(
            scaled, projector, precision=lax.Precision.HIGHEST, preferred_element_type=jnp.float32
        )
        return kinetic_v + potential * field + nonlocal_v.reshape(field.shape)

    previous = states
    current = (apply_h(states) - filter_centre * states) / filter_half
    for degree_k in range(1, DEGREE):
        following = 2.0 * (apply_h(current) - filter_centre * current) / filter_half - previous
        previous = current
        current = following
    images = apply_h(current)
    flat_y = current.reshape(state_count, points)
    flat_h = images.reshape(state_count, points)
    total_points = float(points * lax.axis_size("grid"))
    gathered = lax.all_gather(flat_y, "band", axis=0, tiled=True)
    partial_blocks = jnp.stack([inner_rows(flat_y, gathered), inner_rows(flat_h, gathered)])
    blocks = lax.psum(partial_blocks, "grid")
    gram = blocks[0] / total_points
    hamiltonian = blocks[1] / total_points
    return (current, gram, hamiltonian)


def solution(mesh):
    in_specs = (P("band", "grid", None, None), P("grid", None, None), P(), P(), P())
    out_specs = (P("band", "grid", None, None), P("band", None), P("band", None))
    return jax.shard_map(
        per_device, mesh=mesh, in_specs=in_specs, out_specs=out_specs, check_vma=False
    )
```

profile of v0, /device:TPU:0, one launch (start us, length us, event | category | flops | bytes accessed | tf_op | source)
XLA Modules:
  0.0 211.4 jit_solution(2648983875373184538)
XLA Ops:
  8.4 4.9 %collective-permute-start.1 = (f32[16,4,8,128]{3,2,1,0:T(8,128)S(1)}, f32[16,4,8,128]{3,2,1,0:T(8,128)S(1)}, u32[]{:S(2)}, u32[]{:S(2)}) collective-permute-start(f32[16,4,8,128]{3,2,1,0:T(8,128)S(1)} %get-tuple-element.14), channel_id=1, source_target_pairs={{0,1},{1,2},{2,3},{3,4},{4,5},{5,6},{6,7},{8,9},{9,10},{10,11},{11... | collective-permute-start | bytes 786440 | tf_op jit(solution)/shard_map/ppermute | solution.py:18
  13.3 1.3 collective-permute-start
  17.5 14.1 %scatter_custom_fusion = f32[131072]{0:T(1024)S(1)} fusion(s32[2048]{0:T(1024)S(1)} %select_bitcast_fusion, f32[2048]{0:T(1024)S(1)} %select_bitcast_fusion.1, f32[]{:T(128)} %constant.17.clone.1), kind=kCustom, calls=%fused_computation.348 | custom fusion | flops 2048 | bytes 524292
  32.7 23.2 %psum.42 = f32[16,16]{0,1:T(8,128)S(1)} all-reduce(f32[16,16]{0,1:T(8,128)S(1)} %convolution_bitcast_fusion.5), channel_id=1, replica_groups=mesh['band'=4,'grid'=8] {'grid'}, use_global_device_ids=true, to_apply=%region_1.2 | all-reduce | flops 256 | bytes 2048 | tf_op jit(solution)/shard_map/psum | solution.py:88
  56.9 1.2 broadcast_multiply_fusion
  58.8 1.3 collective-permute-start.3
  60.1 1.3 collective-permute-start.2
  62.4 20.4 %psum.43 = f32[16,16]{0,1:T(8,128)S(1)} all-reduce(f32[16,16]{0,1:T(8,128)S(1)} %fusion.189), channel_id=1, replica_groups=mesh['band'=4,'grid'=8] {'grid'}, use_global_device_ids=true, to_apply=%region_2.3 | all-reduce | flops 256 | bytes 2048 | tf_op jit(solution)/shard_map/psum | solution.py:88
  83.6 1.3 fusion.113
  85.0 1.3 collective-permute-start.5
  86.3 1.3 collective-permute-start.4
  88.6 20.4 %psum.44 = f32[16,16]{0,1:T(8,128)S(1)} all-reduce(f32[16,16]{0,1:T(8,128)S(1)} %fusion.186), channel_id=1, replica_groups=mesh['band'=4,'grid'=8] {'grid'}, use_global_device_ids=true, to_apply=%region_3.4 | all-reduce | flops 256 | bytes 2048 | tf_op jit(solution)/shard_map/psum | solution.py:88
  109.8 1.3 fusion.79
  111.1 1.7 collective-permute-start.7
  112.8 1.3 collective-permute-start.6
  115.1 20.2 %psum.45 = f32[16,16]{0,1:T(8,128)S(1)} all-reduce(f32[16,16]{0,1:T(8,128)S(1)} %fusion.183), channel_id=1, replica_groups=mesh['band'=4,'grid'=8] {'grid'}, use_global_device_ids=true, to_apply=%region_4.5 | all-reduce | flops 256 | bytes 2048 | tf_op jit(solution)/shard_map/psum | solution.py:88
  136.2 1.3 fusion.45
  138.7 1.5 collective-permute-start.9
  140.2 1.3 collective-permute-start.8
  142.4 21.0 %psum.46 = f32[16,16]{0,1:T(8,128)S(1)} all-reduce(f32[16,16]{0,1:T(8,128)S(1)} %fusion.213), channel_id=1, replica_groups=mesh['band'=4,'grid'=8] {'grid'}, use_global_device_ids=true, to_apply=%region_5.6 | all-reduce | flops 256 | bytes 2048 | tf_op jit(solution)/shard_map/psum | solution.py:88
  164.3 1.3 fusion.11
  165.6 3.5 %convolution_bitcast_fusion.7 = f32[1,16,64]{2,1,0:T(8,128)S(1)} fusion(f32[64,8192]{1,0:T(8,128)} %all-gather.2.cloned.1.call-done, f32[2,8,64,128]{3,2,1,0:T(8,128)S(1)} %bitcast.82), kind=kOutput, calls=%fused_computation.112 | convolution fusion | flops 100663296 | bytes 2625536 | tf_op jit(solution)/shard_map/dot_general | solution.py:62
  169.1 1.7 convolution_bitcast_fusion.6
  170.8 33.1 %psum.47 = f32[2,16,64]{2,1,0:T(8,128)S(1)} all-reduce(f32[2,16,64]{2,1,0:T(8,128)S(1)} %pad_maximum_fusion.8), channel_id=1, replica_groups=mesh['band'=4,'grid'=8] {'grid'}, use_global_device_ids=true, to_apply=%region_6.7 | all-reduce | flops 2048 | bytes 16384 | tf_op jit(solution)/shard_map/psum | solution.py:107
  (57 shorter events, 15.8 us)
Async XLA Ops:
  7.2 24.6 %copy-start.1 = (f32[16,8,8,128]{3,2,1,0:T(8,128)S(1)}, f32[16,8,8,128]{3,2,1,0:T(8,128)}, u32[]{:S(2)}) copy-start(f32[16,8,8,128]{3,2,1,0:T(8,128)} %param.5) | copy-start | bytes 1572868
  7.2 48.7 %copy-start.3 = (f32[8,8,128]{2,1,0:T(8,128)S(1)}, f32[8,8,128]{2,1,0:T(8,128)}, u32[]{:S(2)}) copy-start(f32[8,8,128]{2,1,0:T(8,128)} %param.6) | copy-start | bytes 98308
  7.2 48.7 %copy-start.4 = (f32[16]{0:T(128)S(1)}, f32[16]{0:T(128)}, u32[]{:S(2)}) copy-start(f32[16]{0:T(128)} %param.9) | copy-start | bytes 196
  7.2 158.4 %all-gather.2.cloned.1.call-start = ((), (), s32[]{:S(2)}) async-start(), calls=%async_computation | async-start | bytes 2621440 | tf_op jit(solution)/shard_map/all_gather | solution.py:105
  8.4 48.3 %collective-permute-start.1 = (f32[16,4,8,128]{3,2,1,0:T(8,128)S(1)}, f32[16,4,8,128]{3,2,1,0:T(8,128)S(1)}, u32[]{:S(2)}, u32[]{:S(2)}) collective-permute-start(f32[16,4,8,128]{3,2,1,0:T(8,128)S(1)} %get-tuple-element.14), channel_id=1, source_target_pairs={{0,1},{1,2},{2,3},{3,4},{4,5},{5,6},{6,7},{8,9},{9,10},{10,11},{11... | collective-permute-start | bytes 786440 | tf_op jit(solution)/shard_map/ppermute | solution.py:18
  13.3 43.6 %collective-permute-start = (f32[16,4,8,128]{3,2,1,0:T(8,128)S(1)}, f32[16,4,8,128]{3,2,1,0:T(8,128)S(1)}, u32[]{:S(2)}, u32[]{:S(2)}) collective-permute-start(f32[16,4,8,128]{3,2,1,0:T(8,128)S(1)} %get-tuple-element.13), channel_id=1, source_target_pairs={{1,0},{2,1},{3,2},{4,3},{5,4},{6,5},{7,6},{9,8},{10,9},{11,10},{12... | collective-permute-start | bytes 786440 | tf_op jit(solution)/shard_map/ppermute | solution.py:21
  58.8 24.8 %collective-permute-start.3 = (f32[16,4,8,128]{3,2,1,0:T(8,128)}, f32[16,4,8,128]{3,2,1,0:T(8,128)S(1)}, u32[]{:S(2)}, u32[]{:S(2)}) collective-permute-start(f32[16,4,8,128]{3,2,1,0:T(8,128)} %get-tuple-element.12), channel_id=1, source_target_pairs={{0,1},{1,2},{2,3},{3,4},{4,5},{5,6},{6,7},{8,9},{9,10},{10,11},{11... | collective-permute-start | bytes 786440 | tf_op jit(solution)/shard_map/ppermute | solution.py:18
  60.1 23.5 %collective-permute-start.2 = (f32[16,4,8,128]{3,2,1,0:T(8,128)S(1)}, f32[16,4,8,128]{3,2,1,0:T(8,128)S(1)}, u32[]{:S(2)}, u32[]{:S(2)}) collective-permute-start(f32[16,4,8,128]{3,2,1,0:T(8,128)S(1)} %get-tuple-element.11), channel_id=1, source_target_pairs={{1,0},{2,1},{3,2},{4,3},{5,4},{6,5},{7,6},{9,8},{10,9},{11,10},{12... | collective-permute-start | bytes 786440 | tf_op jit(solution)/shard_map/ppermute | solution.py:21
  85.0 24.8 %collective-permute-start.5 = (f32[16,4,8,128]{3,2,1,0:T(8,128)S(1)}, f32[16,4,8,128]{3,2,1,0:T(8,128)S(1)}, u32[]{:S(2)}, u32[]{:S(2)}) collective-permute-start(f32[16,4,8,128]{3,2,1,0:T(8,128)S(1)} %get-tuple-element.10), channel_id=1, source_target_pairs={{0,1},{1,2},{2,3},{3,4},{4,5},{5,6},{6,7},{8,9},{9,10},{10,11},{11... | collective-permute-start | bytes 786440 | tf_op jit(solution)/shard_map/ppermute | solution.py:18
  86.3 23.5 %collective-permute-start.4 = (f32[16,4,8,128]{3,2,1,0:T(8,128)S(1)}, f32[16,4,8,128]{3,2,1,0:T(8,128)S(1)}, u32[]{:S(2)}, u32[]{:S(2)}) collective-permute-start(f32[16,4,8,128]{3,2,1,0:T(8,128)S(1)} %get-tuple-element.9), channel_id=1, source_target_pairs={{1,0},{2,1},{3,2},{4,3},{5,4},{6,5},{7,6},{9,8},{10,9},{11,10},{12... | collective-permute-start | bytes 786440 | tf_op jit(solution)/shard_map/ppermute | solution.py:21
  111.1 25.1 %collective-permute-start.7 = (f32[16,4,8,128]{3,2,1,0:T(8,128)S(1)}, f32[16,4,8,128]{3,2,1,0:T(8,128)S(1)}, u32[]{:S(2)}, u32[]{:S(2)}) collective-permute-start(f32[16,4,8,128]{3,2,1,0:T(8,128)S(1)} %get-tuple-element.8), channel_id=1, source_target_pairs={{0,1},{1,2},{2,3},{3,4},{4,5},{5,6},{6,7},{8,9},{9,10},{10,11},{11... | collective-permute-start | bytes 786440 | tf_op jit(solution)/shard_map/ppermute | solution.py:18
  112.8 23.3 %collective-permute-start.6 = (f32[16,4,8,128]{3,2,1,0:T(8,128)S(1)}, f32[16,4,8,128]{3,2,1,0:T(8,128)S(1)}, u32[]{:S(2)}, u32[]{:S(2)}) collective-permute-start(f32[16,4,8,128]{3,2,1,0:T(8,128)S(1)} %get-tuple-element.7), channel_id=1, source_target_pairs={{1,0},{2,1},{3,2},{4,3},{5,4},{6,5},{7,6},{9,8},{10,9},{11,10},{12... | collective-permute-start | bytes 786440 | tf_op jit(solution)/shard_map/ppermute | solution.py:21
  137.5 28.1 %copy-start = (f32[16,8,8,128]{3,2,1,0:T(8,128)}, f32[16,8,8,128]{3,2,1,0:T(8,128)S(1)}, u32[]{:S(2)}) copy-start(f32[16,8,8,128]{3,2,1,0:T(8,128)S(1)} %fusion.45) | copy-start | bytes 1572868
  138.7 25.6 %collective-permute-start.9 = (f32[16,4,8,128]{3,2,1,0:T(8,128)S(1)}, f32[16,4,8,128]{3,2,1,0:T(8,128)S(1)}, u32[]{:S(2)}, u32[]{:S(2)}) collective-permute-start(f32[16,4,8,128]{3,2,1,0:T(8,128)S(1)} %get-tuple-element.6), channel_id=1, source_target_pairs={{0,1},{1,2},{2,3},{3,4},{4,5},{5,6},{6,7},{8,9},{9,10},{10,11},{11... | collective-permute-start | bytes 786440 | tf_op jit(solution)/shard_map/ppermute | solution.py:18
  140.2 24.1 %collective-permute-start.8 = (f32[16,4,8,128]{3,2,1,0:T(8,128)S(1)}, f32[16,4,8,128]{3,2,1,0:T(8,128)S(1)}, u32[]{:S(2)}, u32[]{:S(2)}) collective-permute-start(f32[16,4,8,128]{3,2,1,0:T(8,128)S(1)} %get-tuple-element.5), channel_id=1, source_target_pairs={{1,0},{2,1},{3,2},{4,3},{5,4},{6,5},{7,6},{9,8},{10,9},{11,10},{12... | collective-permute-start | bytes 786440 | tf_op jit(solution)/shard_map/ppermute | solution.py:21
  165.6 3.5 %copy-start.2 = (f32[64,8192]{1,0:T(8,128)S(1)}, f32[64,8192]{1,0:T(8,128)}, u32[]{:S(2)}) copy-start(f32[64,8192]{1,0:T(8,128)} %all-gather.2.cloned.1.call-done) | copy-start | bytes 6291460
Sparse Core Ops, SparseCore 0:
  138.7 20.3 all-gather.1
where the time goes:
time: 212 us; the launch traced here: 211 us
  blocking collectives  138 us (65%)
  other arithmetic  23.9 us (11%)
  starting transfers between devices  17.2 us (8%)
  between operations  14.5 us (7%)
  matrix products  13.6 us (6%)
  local copies, waits for them, and re-layouts  3.87 us (2%)
    psum x5, blocking collectives, apply_h(): coeffs = lax.psum(partial_value, 'grid')  105 us
    psum x1, blocking collectives, per_device(): blocks = lax.psum(partial_blocks, 'grid')  33.1 us
    unnamed x4, other arithmetic  15.6 us
    ppermute x5, starting transfers between devices, padded_2(): lax.ppermute(lax.slice_in_dim(block, block.shape[dim] - width, None, axis...  10.7 us
    dot_general x7, matrix products, inner_rows(): lax.dot_general(left, right, (((1,), (1,)), ((), ())), precision=lax.Prec...  10.1 us
    ppermute x5, starting transfers between devices, padded_2(): lax.ppermute(lax.slice_in_dim(block, 0, width, axis=dim), axis, backward)  6.46 us
  transfers between devices with their start and end apart: 11, of which 0 were waited for; matrix products, arithmetic and copies ran while one was open for 13% of the time, Pallas kernels for 0%

commit v1 on v0

--- a/solution.py
+++ b/solution.py
@@ -85,7 +85,8 @@
         kinetic_v = kinetic(padded)
         flat_v = field.reshape(state_count, points)
         partial_value = inner_rows(flat_v, projector)
-        coeffs = lax.psum(partial_value, "grid")
+        terms = lax.all_gather(partial_value, "grid", axis=0, tiled=False)
+        coeffs = terms.sum(axis=0)
         scaled = coeffs * proj_strength[None, :]
         nonlocal_v = jnp.dot(
             scaled, projector, precision=lax.Precision.HIGHEST, preferred_element_type=jnp.float32

time: 212 us -> 278 us (1.31)
  blocking collectives: 138 us -> 195 us
  starting transfers between devices: 17.2 us -> 26.7 us
    all_gather x0 -> x5, blocking collectives: none -> 157 us  [apply_h(): terms = lax.all_gather(partial_value, 'grid', axis=0, tiled=False)]
    psum x5 -> x0, blocking collectives: 105 us -> none  [apply_h(): coeffs = lax.psum(partial_value, 'grid')]
    ppermute x5, starting transfers between devices: 10.7 us -> 20.2 us  [padded_2(): lax.ppermute(lax.slice_in_dim(block, block.shape[dim] - width, None, axis...]
    psum x1, blocking collectives: 33.1 us -> 37.6 us  [per_device(): blocks = lax.psum(partial_blocks, 'grid')]
  transfers between devices with their start and end apart: 11 -> 11, of which waited for: 0 -> 0; matrix products, arithmetic and copies ran while one was open for 13% -> 10% of each run, Pallas kernels for 0% -> 0%
where the time goes in v1:
time: 278 us
  blocking collectives  195 us (70%)
  starting transfers between devices  26.7 us (10%)
  other arithmetic  24 us (9%)
  between operations  14.5 us (5%)
  matrix products  13.5 us (5%)
  local copies, waits for them, and re-layouts  4.31 us (2%)
    all_gather x5, blocking collectives, apply_h(): terms = lax.all_gather(partial_value, 'grid', axis=0, tiled=False)  157 us
    psum x1, blocking collectives, per_device(): blocks = lax.psum(partial_blocks, 'grid')  37.6 us
    ppermute x5, starting transfers between devices, padded_2(): lax.ppermute(lax.slice_in_dim(block, block.shape[dim] - width, None, axis...  20.2 us
    unnamed x4, other arithmetic  15.6 us
    dot_general x7, matrix products, inner_rows(): lax.dot_general(left, right, (((1,), (1,)), ((), ())), precision=lax.Prec...  10 us
    ppermute x5, starting transfers between devices, padded_2(): lax.ppermute(lax.slice_in_dim(block, 0, width, axis=dim), axis, backward)  6.46 us
  transfers between devices with their start and end apart: 11, of which 0 were waited for; matrix products, arithmetic and copies ran while one was open for 10% of the time, Pallas kernels for 0%

profile of v1, /device:TPU:0, one launch (start us, length us, event | category | flops | bytes accessed | tf_op | source)
XLA Modules:
  0.0 277.7 jit_solution(1272269853869877625)
XLA Ops:
  8.4 4.9 %collective-permute-start.1 = (f32[16,4,8,128]{3,2,1,0:T(8,128)S(1)}, f32[16,4,8,128]{3,2,1,0:T(8,128)S(1)}, u32[]{:S(2)}, u32[]{:S(2)}) collective-permute-start(f32[16,4,8,128]{3,2,1,0:T(8,128)S(1)} %get-tuple-element.14), channel_id=1, source_target_pairs={{0,1},{1,2},{2,3},{3,4},{4,5},{5,6},{6,7},{8,9},{9,10},{10,11},{11... | collective-permute-start | bytes 786440 | tf_op jit(solution)/shard_map/ppermute | solution.py:18
  13.3 1.3 collective-permute-start
  17.5 14.1 %scatter_custom_fusion = f32[131072]{0:T(1024)S(1)} fusion(s32[2048]{0:T(1024)S(1)} %select_bitcast_fusion, f32[2048]{0:T(1024)S(1)} %select_bitcast_fusion.1, f32[]{:T(128)} %constant.17.clone.1), kind=kCustom, calls=%fused_computation.348 | custom fusion | flops 2048 | bytes 524292
  32.8 32.1 %all-gather = f32[128,16]{1,0:T(8,128)S(1)} all-gather(f32[16,16]{1,0:T(8,128)S(1)} %copy.10), channel_id=2, replica_groups=mesh['band'=4,'grid'=8] {'grid'}, dimensions={0}, use_global_device_ids=true | all-gather | bytes 9216 | tf_op jit(solution)/shard_map/all_gather | solution.py:88
  66.0 1.2 broadcast_multiply_fusion
  67.9 3.4 %collective-permute-start.3 = (f32[16,4,8,128]{3,2,1,0:T(8,128)}, f32[16,4,8,128]{3,2,1,0:T(8,128)S(1)}, u32[]{:S(2)}, u32[]{:S(2)}) collective-permute-start(f32[16,4,8,128]{3,2,1,0:T(8,128)} %get-tuple-element.12), channel_id=1, source_target_pairs={{0,1},{1,2},{2,3},{3,4},{4,5},{5,6},{6,7},{8,9},{9,10},{10,11},{11... | collective-permute-start | bytes 786440 | tf_op jit(solution)/shard_map/ppermute | solution.py:18
  71.3 1.3 collective-permute-start.2
  73.6 31.3 %all-gather.1 = f32[128,16]{1,0:T(8,128)S(1)} all-gather(f32[16,16]{1,0:T(8,128)S(1)} %fusion.189), channel_id=3, replica_groups=mesh['band'=4,'grid'=8] {'grid'}, dimensions={0}, use_global_device_ids=true | all-gather | bytes 9216 | tf_op jit(solution)/shard_map/all_gather | solution.py:88
  105.8 1.3 fusion.113
  107.1 3.9 %collective-permute-start.5 = (f32[16,4,8,128]{3,2,1,0:T(8,128)S(1)}, f32[16,4,8,128]{3,2,1,0:T(8,128)S(1)}, u32[]{:S(2)}, u32[]{:S(2)}) collective-permute-start(f32[16,4,8,128]{3,2,1,0:T(8,128)S(1)} %get-tuple-element.10), channel_id=1, source_target_pairs={{0,1},{1,2},{2,3},{3,4},{4,5},{5,6},{6,7},{8,9},{9,10},{10,11},{11... | collective-permute-start | bytes 786440 | tf_op jit(solution)/shard_map/ppermute | solution.py:18
  111.1 1.3 collective-permute-start.4
  113.3 31.2 %all-gather.2 = f32[128,16]{1,0:T(8,128)S(1)} all-gather(f32[16,16]{1,0:T(8,128)S(1)} %fusion.186), channel_id=4, replica_groups=mesh['band'=4,'grid'=8] {'grid'}, dimensions={0}, use_global_device_ids=true | all-gather | bytes 9216 | tf_op jit(solution)/shard_map/all_gather | solution.py:88
  145.5 1.3 fusion.79
  146.8 4.0 %collective-permute-start.7 = (f32[16,4,8,128]{3,2,1,0:T(8,128)S(1)}, f32[16,4,8,128]{3,2,1,0:T(8,128)S(1)}, u32[]{:S(2)}, u32[]{:S(2)}) collective-permute-start(f32[16,4,8,128]{3,2,1,0:T(8,128)S(1)} %get-tuple-element.8), channel_id=1, source_target_pairs={{0,1},{1,2},{2,3},{3,4},{4,5},{5,6},{6,7},{8,9},{9,10},{10,11},{11... | collective-permute-start | bytes 786440 | tf_op jit(solution)/shard_map/ppermute | solution.py:18
  150.8 1.3 collective-permute-start.6
  153.0 31.3 %all-gather.3 = f32[128,16]{1,0:T(8,128)S(1)} all-gather(f32[16,16]{1,0:T(8,128)S(1)} %fusion.183), channel_id=5, replica_groups=mesh['band'=4,'grid'=8] {'grid'}, dimensions={0}, use_global_device_ids=true | all-gather | bytes 9216 | tf_op jit(solution)/shard_map/all_gather | solution.py:88
  185.3 1.3 fusion.45
  187.8 3.9 %collective-permute-start.9 = (f32[16,4,8,128]{3,2,1,0:T(8,128)S(1)}, f32[16,4,8,128]{3,2,1,0:T(8,128)S(1)}, u32[]{:S(2)}, u32[]{:S(2)}) collective-permute-start(f32[16,4,8,128]{3,2,1,0:T(8,128)S(1)} %get-tuple-element.6), channel_id=1, source_target_pairs={{0,1},{1,2},{2,3},{3,4},{4,5},{5,6},{6,7},{8,9},{9,10},{10,11},{11... | collective-permute-start | bytes 786440 | tf_op jit(solution)/shard_map/ppermute | solution.py:18
  191.7 1.3 collective-permute-start.8
  194.0 31.1 %all-gather.4 = f32[128,16]{1,0:T(8,128)S(1)} all-gather(f32[16,16]{1,0:T(8,128)S(1)} %fusion.213), channel_id=6, replica_groups=mesh['band'=4,'grid'=8] {'grid'}, dimensions={0}, use_global_device_ids=true | all-gather | bytes 9216 | tf_op jit(solution)/shard_map/all_gather | solution.py:88
  226.1 1.3 fusion.11
  227.4 3.5 %convolution_bitcast_fusion.7 = f32[1,16,64]{2,1,0:T(8,128)S(1)} fusion(f32[64,8192]{1,0:T(8,128)} %all-gather.7.cloned.1.call-done, f32[2,8,64,128]{3,2,1,0:T(8,128)S(1)} %bitcast.87), kind=kOutput, calls=%fused_computation.112 | convolution fusion | flops 100663296 | bytes 2625536 | tf_op jit(solution)/shard_map/dot_general | solution.py:62
  230.9 1.7 convolution_bitcast_fusion.6
  232.7 37.6 %psum.7 = f32[2,16,64]{2,1,0:T(8,128)S(1)} all-reduce(f32[2,16,64]{2,1,0:T(8,128)S(1)} %pad_maximum_fusion.8), channel_id=1, replica_groups=mesh['band'=4,'grid'=8] {'grid'}, use_global_device_ids=true, to_apply=%region_6.7 | all-reduce | flops 2048 | bytes 16384 | tf_op jit(solution)/shard_map/psum | solution.py:108
  (68 shorter events, 16.3 us)
Async XLA Ops:
  7.2 24.6 %copy-start.1 = (f32[16,8,8,128]{3,2,1,0:T(8,128)S(1)}, f32[16,8,8,128]{3,2,1,0:T(8,128)}, u32[]{:S(2)}) copy-start(f32[16,8,8,128]{3,2,1,0:T(8,128)} %param.5) | copy-start | bytes 1572868
  7.2 57.8 %copy-start.3 = (f32[8,8,128]{2,1,0:T(8,128)S(1)}, f32[8,8,128]{2,1,0:T(8,128)}, u32[]{:S(2)}) copy-start(f32[8,8,128]{2,1,0:T(8,128)} %param.6) | copy-start | bytes 98308
  7.2 57.8 %copy-start.4 = (f32[16]{0:T(128)S(1)}, f32[16]{0:T(128)}, u32[]{:S(2)}) copy-start(f32[16]{0:T(128)} %param.9) | copy-start | bytes 196
  7.2 220.2 %all-gather.7.cloned.1.call-start = ((), (), s32[]{:S(2)}) async-start(), calls=%async_computation | async-start | bytes 2621440 | tf_op jit(solution)/shard_map/all_gather | solution.py:106
  8.4 57.4 %collective-permute-start.1 = (f32[16,4,8,128]{3,2,1,0:T(8,128)S(1)}, f32[16,4,8,128]{3,2,1,0:T(8,128)S(1)}, u32[]{:S(2)}, u32[]{:S(2)}) collective-permute-start(f32[16,4,8,128]{3,2,1,0:T(8,128)S(1)} %get-tuple-element.14), channel_id=1, source_target_pairs={{0,1},{1,2},{2,3},{3,4},{4,5},{5,6},{6,7},{8,9},{9,10},{10,11},{11... | collective-permute-start | bytes 786440 | tf_op jit(solution)/shard_map/ppermute | solution.py:18
  13.3 52.7 %collective-permute-start = (f32[16,4,8,128]{3,2,1,0:T(8,128)S(1)}, f32[16,4,8,128]{3,2,1,0:T(8,128)S(1)}, u32[]{:S(2)}, u32[]{:S(2)}) collective-permute-start(f32[16,4,8,128]{3,2,1,0:T(8,128)S(1)} %get-tuple-element.13), channel_id=1, source_target_pairs={{1,0},{2,1},{3,2},{4,3},{5,4},{6,5},{7,6},{9,8},{10,9},{11,10},{12... | collective-permute-start | bytes 786440 | tf_op jit(solution)/shard_map/ppermute | solution.py:21
  67.9 37.9 %collective-permute-start.3 = (f32[16,4,8,128]{3,2,1,0:T(8,128)}, f32[16,4,8,128]{3,2,1,0:T(8,128)S(1)}, u32[]{:S(2)}, u32[]{:S(2)}) collective-permute-start(f32[16,4,8,128]{3,2,1,0:T(8,128)} %get-tuple-element.12), channel_id=1, source_target_pairs={{0,1},{1,2},{2,3},{3,4},{4,5},{5,6},{6,7},{8,9},{9,10},{10,11},{11... | collective-permute-start | bytes 786440 | tf_op jit(solution)/shard_map/ppermute | solution.py:18
  71.3 34.4 %collective-permute-start.2 = (f32[16,4,8,128]{3,2,1,0:T(8,128)S(1)}, f32[16,4,8,128]{3,2,1,0:T(8,128)S(1)}, u32[]{:S(2)}, u32[]{:S(2)}) collective-permute-start(f32[16,4,8,128]{3,2,1,0:T(8,128)S(1)} %get-tuple-element.11), channel_id=1, source_target_pairs={{1,0},{2,1},{3,2},{4,3},{5,4},{6,5},{7,6},{9,8},{10,9},{11,10},{12... | collective-permute-start | bytes 786440 | tf_op jit(solution)/shard_map/ppermute | solution.py:21
  107.1 38.3 %collective-permute-start.5 = (f32[16,4,8,128]{3,2,1,0:T(8,128)S(1)}, f32[16,4,8,128]{3,2,1,0:T(8,128)S(1)}, u32[]{:S(2)}, u32[]{:S(2)}) collective-permute-start(f32[16,4,8,128]{3,2,1,0:T(8,128)S(1)} %get-tuple-element.10), channel_id=1, source_target_pairs={{0,1},{1,2},{2,3},{3,4},{4,5},{5,6},{6,7},{8,9},{9,10},{10,11},{11... | collective-permute-start | bytes 786440 | tf_op jit(solution)/shard_map/ppermute | solution.py:18
  111.1 34.4 %collective-permute-start.4 = (f32[16,4,8,128]{3,2,1,0:T(8,128)S(1)}, f32[16,4,8,128]{3,2,1,0:T(8,128)S(1)}, u32[]{:S(2)}, u32[]{:S(2)}) collective-permute-start(f32[16,4,8,128]{3,2,1,0:T(8,128)S(1)} %get-tuple-element.9), channel_id=1, source_target_pairs={{1,0},{2,1},{3,2},{4,3},{5,4},{6,5},{7,6},{9,8},{10,9},{11,10},{12... | collective-permute-start | bytes 786440 | tf_op jit(solution)/shard_map/ppermute | solution.py:21
  146.8 38.5 %collective-permute-start.7 = (f32[16,4,8,128]{3,2,1,0:T(8,128)S(1)}, f32[16,4,8,128]{3,2,1,0:T(8,128)S(1)}, u32[]{:S(2)}, u32[]{:S(2)}) collective-permute-start(f32[16,4,8,128]{3,2,1,0:T(8,128)S(1)} %get-tuple-element.8), channel_id=1, source_target_pairs={{0,1},{1,2},{2,3},{3,4},{4,5},{5,6},{6,7},{8,9},{9,10},{10,11},{11... | collective-permute-start | bytes 786440 | tf_op jit(solution)/shard_map/ppermute | solution.py:18
  150.8 34.5 %collective-permute-start.6 = (f32[16,4,8,128]{3,2,1,0:T(8,128)S(1)}, f32[16,4,8,128]{3,2,1,0:T(8,128)S(1)}, u32[]{:S(2)}, u32[]{:S(2)}) collective-permute-start(f32[16,4,8,128]{3,2,1,0:T(8,128)S(1)} %get-tuple-element.7), channel_id=1, source_target_pairs={{1,0},{2,1},{3,2},{4,3},{5,4},{6,5},{7,6},{9,8},{10,9},{11,10},{12... | collective-permute-start | bytes 786440 | tf_op jit(solution)/shard_map/ppermute | solution.py:21
  186.6 40.8 %copy-start = (f32[16,8,8,128]{3,2,1,0:T(8,128)}, f32[16,8,8,128]{3,2,1,0:T(8,128)S(1)}, u32[]{:S(2)}) copy-start(f32[16,8,8,128]{3,2,1,0:T(8,128)S(1)} %fusion.45) | copy-start | bytes 1572868
  187.8 38.3 %collective-permute-start.9 = (f32[16,4,8,128]{3,2,1,0:T(8,128)S(1)}, f32[16,4,8,128]{3,2,1,0:T(8,128)S(1)}, u32[]{:S(2)}, u32[]{:S(2)}) collective-permute-start(f32[16,4,8,128]{3,2,1,0:T(8,128)S(1)} %get-tuple-element.6), channel_id=1, source_target_pairs={{0,1},{1,2},{2,3},{3,4},{4,5},{5,6},{6,7},{8,9},{9,10},{10,11},{11... | collective-permute-start | bytes 786440 | tf_op jit(solution)/shard_map/ppermute | solution.py:18
  191.7 34.3 %collective-permute-start.8 = (f32[16,4,8,128]{3,2,1,0:T(8,128)S(1)}, f32[16,4,8,128]{3,2,1,0:T(8,128)S(1)}, u32[]{:S(2)}, u32[]{:S(2)}) collective-permute-start(f32[16,4,8,128]{3,2,1,0:T(8,128)S(1)} %get-tuple-element.5), channel_id=1, source_target_pairs={{1,0},{2,1},{3,2},{4,3},{5,4},{6,5},{7,6},{9,8},{10,9},{11,10},{12... | collective-permute-start | bytes 786440 | tf_op jit(solution)/shard_map/ppermute | solution.py:21
  227.4 3.5 %copy-start.2 = (f32[64,8192]{1,0:T(8,128)S(1)}, f32[64,8192]{1,0:T(8,128)}, u32[]{:S(2)}) copy-start(f32[64,8192]{1,0:T(8,128)} %all-gather.7.cloned.1.call-done) | copy-start | bytes 6291460
Sparse Core Ops, SparseCore 0:
  187.9 23.9 all-gather.6
